TPU v7x, 256 devices: a whole 4x4x8 slice. The times are simulated.
256 devices in a mesh: chain: 4 (over y), block: 64 (over x, z, core).
Axes of the slice: x: 4, y: 4, z: 8, core: 2. Of those that a mesh axis runs over, the one named last changes fastest.
Arguments:
- site_blocks: bfloat16 [4, 4, 8192, 2, 128], P('chain', None, 'block'), may hold values from -0.5 to 0.5
- left_carry: bfloat16 [4, 8192, 5, 128], P(None, 'block'), may hold values from -6 to 6
- mpo: float32 [4, 5, 5, 2, 2], replicated, may hold values from -3 to 3
- sketch: bfloat16 [4, 64, 640, 128], P('chain', 'block'), may hold values from -0.25 to 0.25
- ranks: int32 [4, 64], P(None, 'block'), may hold values from 32 to 128, as said below
Outputs:
- new_sites: bfloat16 [4, 4, 8192, 2, 128], P('chain', None, 'block')
- carries: bfloat16 [4, 4, 8192, 5, 128], P('chain', None, 'block')
Inputs may be any that keep to these rules, and one draw needn't show every extreme that they name: Every site has the same ranks; sector 0 keeps 128 // 4 to 64 columns, the top sector 64 - 1 keeps all 128, every other sector 128 // 2 or more.
All inputs are finite; a program needn't handle non-finite values.
Results may differ from a plain program's by a relative error of at most 0.03.
Values may be sent and summed in bfloat16 or wider, within the bound.
A program may use at most 64 MiB of HBM per device.

v0:
```python
import jax
import jax.numpy as jnp
from jax import lax
from jax.sharding import PartitionSpec as P

CHARGES = (0, 1, -1, 0, 0)


def from_behind(x, axis, by):
    length = lax.axis_size(axis)
    pairs = [(i, i + by) for i in range(length) if 0 <= i + by < length]
    return lax.ppermute(x, axis, pairs)


def extended(cells, sides, width):
    for axis, dim in sides:
        count = lax.axis_size(axis)
        ends = count - 1
        head = lax.slice_in_dim(cells, 0, width, axis=dim)
        tail = lax.slice_in_dim(cells, cells.shape[dim] - width, cells.shape[dim], axis=dim)
        cells = jnp.concatenate(
            [
                lax.ppermute(tail, axis, [(i, (i + 1) % count) for i in range(ends)]),
                cells,
                lax.ppermute(head, axis, [((i + 1) % count, i) for i in range(ends)]),
            ],
            axis=dim,
        )
    return cells


def rule_mask():
    charges = jnp.array(CHARGES, dtype=jnp.int32)
    physical = jnp.arange(2, dtype=jnp.int32)
    state_change = physical[None, None, :, None] - physical[None, None, None, :]
    charge_change = charges[None, :, None, None] - charges[:, None, None, None]
    return (state_change == charge_change).astype(jnp.float32)


def solve_lower(factor, right_side):
    return jax.scipy.linalg.solve_triangular(factor, right_side.T, lower=True)


def site_step(carried, neighbours, coupled, sketch_site, kept_rank):
    state_count = carried.shape[0]
    sector_width = carried.shape[1]
    channel_count = carried.shape[2]
    selected = jnp.stack(
        [
            neighbours[:, (1 - charge_value) * sector_width : (2 - charge_value) * sector_width]
            for charge_value in CHARGES
        ],
        axis=1,
    )
    products = jnp.einsum(
        "aiwj,awjsk->aiwsk", carried, selected, preferred_element_type=jnp.float32
    )
    contracted = jnp.einsum(
        "wvts,aiwsk->ativk", coupled, products, precision=lax.Precision.HIGHEST
    ).astype(jnp.bfloat16)
    from_below = from_behind(contracted[:, 1], "block", 1)
    column_count = channel_count * sector_width
    stacked = jnp.concatenate(
        [
            contracted[:, 0].reshape(state_count, sector_width, column_count),
            from_below.reshape(state_count, sector_width, column_count),
        ],
        axis=1,
    )
    sketched = jnp.einsum("arc,cj->arj", stacked, sketch_site, preferred_element_type=jnp.float32)
    kept_cols = (jnp.arange(sector_width, dtype=jnp.int32) < kept_rank).astype(jnp.float32)
    sketched = sketched * kept_cols
    gram_matrix = jnp.einsum("arj,arl->ajl", sketched, sketched, precision=lax.Precision.HIGHEST)
    diag_terms = sector_width / 4.0 * kept_cols + (1.0 - kept_cols)
    gram_matrix = gram_matrix + jnp.eye(sector_width, dtype=jnp.float32) * diag_terms
    factor = jnp.linalg.cholesky(gram_matrix)
    isometry = jax.vmap(solve_lower)(factor, sketched).astype(jnp.bfloat16)
    carried_next = jnp.einsum("alr,arc->alc", isometry, stacked, preferred_element_type=jnp.float32)
    carried_next = carried_next.astype(jnp.bfloat16).reshape(
        state_count, sector_width, channel_count, sector_width
    )
    return (isometry.reshape(state_count, sector_width, 2, sector_width), carried_next)


def per_device(site_blocks, left_carry, mpo, sketch, ranks):
    chain_pos = lax.axis_index("chain")
    block_pos = lax.axis_index("block")
    sectors = lax.axis_size("block")
    sites = lax.axis_size("chain")
    selection = rule_mask()
    local_blocks = site_blocks[0]
    sector_width = local_blocks.shape[1]
    top_mask = jnp.logical_or(block_pos < sectors - 1, jnp.arange(2, dtype=jnp.int32) == 0)
    local_blocks = local_blocks * top_mask.astype(local_blocks.dtype)[None, None, :, None]
    neighbours = extended(local_blocks, (("block", 1),), sector_width)
    site_kept = jnp.zeros(local_blocks.shape, jnp.bfloat16)
    carry_kept = jnp.zeros(left_carry.shape, jnp.bfloat16)
    coupled = mpo[chain_pos] * selection
    sketch_site = sketch[0, 0]
    kept_rank = ranks[chain_pos, 0]
    carried = left_carry
    for step_no in range(sites):
        new_site, carried_next = site_step(carried, neighbours, coupled, sketch_site, kept_rank)
        is_hit = chain_pos == step_no
        site_kept = jnp.where(is_hit, new_site, site_kept)
        carry_kept = jnp.where(is_hit, carried_next, carry_kept)
        if step_no + 1 < sites:
            arrived = from_behind(carried_next, "chain", 1)
            carried = jnp.where(chain_pos == 0, left_carry, arrived)
    return (site_kept[None], carry_kept[None])


def solution(mesh):
    return jax.shard_map(
        per_device,
        mesh=mesh,
        in_specs=(
            P("chain", None, "block", None, None),
            P(None, "block", None, None),
            P(),
            P("chain", "block", None, None),
            P(None, "block"),
        ),
        out_specs=(P("chain", None, "block", None, None), P("chain", None, "block", None, None)),
        check_vma=False,
    )
```

profile of v0, /device:TPU:12, one launch (start us, length us, event | category | flops | bytes accessed | tf_op | source)
XLA Modules:
  0.0 568.0 jit_solution(12815116936908443504)
XLA Ops:
  0.7 1.2 copy.146
  2.0 1.9 collective-permute-start
  3.9 7.2 %collective-permute-start.1 = (bf16[4,128,2,128]{1,3,2,0:T(8,128)(2,1)S(1)}, bf16[4,128,2,128]{1,3,2,0:T(8,128)(2,1)S(1)}, u32[]{:S(2)}, u32[]{:S(2)}) collective-permute-start(bf16[4,128,2,128]{1,3,2,0:T(8,128)(2,1)S(1)} %bitcast_multiply_fusion), channel_id=1, source_target_pairs={{1,0},{2,1},{3,2},{4,3},{5,4},{6,5},{7,6},{8,7},{9,8},{10,9},{11,1... | collective-permute-start | bytes 786440 | tf_op jit(solution)/shard_map/ppermute | solution.py:25
  12.9 1.2 constant_dynamic-slice_fusion
  15.3 2.0 convolution_bitcast_fusion.3
  17.4 5.0 copy.209
  22.3 5.7 %fusion = bf16[4,2,128,5,128]{4,3,1,2,0:T(8,128)(2,1)S(1)} fusion(f32[4,128,5,2,128,1]{4,2,3,5,1,0:T(8,128)} %copy.209, f32[5,5,2,2,1,1]{0,1,3,2,5,4:T(8,128)S(1)} %copy.210), kind=kOutput, calls=%fused_computation.8 | convolution fusion | flops 79298560 | bytes 3932560 | tf_op jit(solution)/shard_map/wvts,aiwsk->ativk/dot_general | solution.py:58
  29.4 2.1 collective-permute-start.2
  33.0 1.3 copy.151
  34.3 2.2 copy.154
  36.4 7.5 %collective-permute-done.2 = bf16[4,128,5,128]{3,1,2,0:T(8,128)(2,1)} collective-permute-done((bf16[4,128,5,128]{3,1,2,0:T(8,128)(2,1)}, bf16[4,128,5,128]{3,1,2,0:T(8,128)(2,1)}, u32[]{:S(2)}, u32[]{:S(2)}) %collective-permute-start.2) | collective-permute-done | bytes 655392 | tf_op jit(solution)/shard_map/ppermute | solution.py:12
  43.9 1.4 copy.153
  45.3 1.1 copy.155
  46.4 1.8 convolution_multiply_fusion.3
  49.5 46.9 %custom-call.12 = f32[4,128,128]{2,1,0:T(8,128)S(1)} custom-call(f32[4,128,128]{2,1,0:T(8,128)S(1)} %fusion.26), custom_call_target="Cholesky" | custom-call | tf_op jit(solution)/shard_map/jit(cholesky)/cholesky | solution.py:76
  96.7 39.3 %custom-call.13 = f32[4,1,128,128]{2,3,1,0:T(8,128)S(1)} custom-call(f32[4,1,128,128]{3,2,1,0:T(8,128)S(1)} %select_bitcast_fusion.3), custom_call_target="InvertDiagBlocksLowerTriangular" | custom-call | tf_op jit(solution)/shard_map/vmap(jit(_solve_triangular))/triangular_solve | solution.py:41
  136.6 1.7 convolution_convert_fusion.3
  138.3 1.1 copy.161
  139.4 3.9 collective-permute-start.3
  143.6 8.5 %collective-permute-done.3 = bf16[4,128,5,128]{1,3,2,0:T(8,128)(2,1)} collective-permute-done((bf16[4,128,5,128]{1,3,2,0:T(8,128)(2,1)}, bf16[4,128,5,128]{1,3,2,0:T(8,128)(2,1)}, u32[]{:S(2)}, u32[]{:S(2)}) %collective-permute-start.3) | collective-permute-done | bytes 655392 | tf_op jit(solution)/shard_map/ppermute | solution.py:12
  152.2 3.1 convolution_bitcast_fusion.2
  155.3 5.0 copy.217
  160.3 5.7 %fusion.1 = bf16[4,2,128,5,128]{4,3,1,2,0:T(8,128)(2,1)S(1)} fusion(f32[4,128,5,2,128,1]{4,2,3,5,1,0:T(8,128)} %copy.217, f32[5,5,2,2,1,1]{0,1,3,2,5,4:T(8,128)S(1)} %copy.210), kind=kOutput, calls=%fused_computation.9 | convolution fusion | flops 79298560 | bytes 3932560 | tf_op jit(solution)/shard_map/wvts,aiwsk->ativk/dot_general | solution.py:58
  167.3 1.9 collective-permute-start.4
  169.3 1.3 copy.166
  170.5 2.2 copy.169
  172.7 9.0 %collective-permute-done.4 = bf16[4,128,5,128]{3,1,2,0:T(8,128)(2,1)} collective-permute-done((bf16[4,128,5,128]{3,1,2,0:T(8,128)(2,1)}, bf16[4,128,5,128]{3,1,2,0:T(8,128)(2,1)}, u32[]{:S(2)}, u32[]{:S(2)}) %collective-permute-start.4) | collective-permute-done | bytes 655392 | tf_op jit(solution)/shard_map/ppermute | solution.py:12
  181.7 1.4 copy.168
  183.1 1.1 copy.170
  184.2 1.8 convolution_multiply_fusion.2
  188.0 47.7 %custom-call.14 = f32[4,128,128]{2,1,0:T(8,128)S(1)} custom-call(f32[4,128,128]{2,1,0:T(8,128)} %fusion.24), custom_call_target="Cholesky" | custom-call | tf_op jit(solution)/shard_map/jit(cholesky)/cholesky | solution.py:76
  235.9 39.9 %custom-call.15 = f32[4,1,128,128]{2,3,1,0:T(8,128)} custom-call(f32[4,1,128,128]{3,2,1,0:T(8,128)S(1)} %select_bitcast_fusion.2), custom_call_target="InvertDiagBlocksLowerTriangular" | custom-call | tf_op jit(solution)/shard_map/vmap(jit(_solve_triangular))/triangular_solve | solution.py:41
  275.9 1.6 convolution_convert_fusion.6
  277.5 2.6 convolution_convert_fusion.2
  280.1 2.2 copy.176
  282.2 3.6 collective-permute-start.5
  285.9 12.5 %collective-permute-done.5 = bf16[4,128,5,128]{1,3,2,0:T(8,128)(2,1)S(1)} collective-permute-done((bf16[4,128,5,128]{1,3,2,0:T(8,128)(2,1)}, bf16[4,128,5,128]{1,3,2,0:T(8,128)(2,1)S(1)}, u32[]{:S(2)}, u32[]{:S(2)}) %collective-permute-start.5) | collective-permute-done | bytes 655392 | tf_op jit(solution)/shard_map/ppermute | solution.py:12
  298.3 2.0 convolution_bitcast_fusion.1
  300.4 5.0 copy.225
  305.3 5.7 %fusion.2 = bf16[4,2,128,5,128]{4,3,1,2,0:T(8,128)(2,1)S(1)} fusion(f32[4,128,5,2,128,1]{4,2,3,5,1,0:T(8,128)} %copy.225, f32[5,5,2,2,1,1]{0,1,3,2,5,4:T(8,128)S(1)} %copy.210), kind=kOutput, calls=%fused_computation.10 | convolution fusion | flops 79298560 | bytes 3932560 | tf_op jit(solution)/shard_map/wvts,aiwsk->ativk/dot_general | solution.py:58
  312.4 1.9 collective-permute-start.6
  314.4 1.3 copy.181
  315.6 2.2 copy.184
  317.8 9.0 %collective-permute-done.6 = bf16[4,128,5,128]{3,1,2,0:T(8,128)(2,1)} collective-permute-done((bf16[4,128,5,128]{3,1,2,0:T(8,128)(2,1)}, bf16[4,128,5,128]{3,1,2,0:T(8,128)(2,1)}, u32[]{:S(2)}, u32[]{:S(2)}) %collective-permute-start.6) | collective-permute-done | bytes 655392 | tf_op jit(solution)/shard_map/ppermute | solution.py:12
  326.8 1.4 copy.183
  328.2 1.1 copy.185
  329.3 1.8 convolution_multiply_fusion.1
  333.0 47.7 %custom-call.16 = f32[4,128,128]{2,1,0:T(8,128)S(1)} custom-call(f32[4,128,128]{2,1,0:T(8,128)} %fusion.22), custom_call_target="Cholesky" | custom-call | tf_op jit(solution)/shard_map/jit(cholesky)/cholesky | solution.py:76
  381.0 39.9 %custom-call.17 = f32[4,1,128,128]{2,3,1,0:T(8,128)} custom-call(f32[4,1,128,128]{3,2,1,0:T(8,128)S(1)} %select_bitcast_fusion.1), custom_call_target="InvertDiagBlocksLowerTriangular" | custom-call | tf_op jit(solution)/shard_map/vmap(jit(_solve_triangular))/triangular_solve | solution.py:41
  420.9 1.6 convolution_convert_fusion.5
  422.5 2.6 convolution_convert_fusion.1
  425.1 2.2 copy.191
  427.3 3.7 collective-permute-start.7
  430.9 12.5 %collective-permute-done.7 = bf16[4,128,5,128]{1,3,2,0:T(8,128)(2,1)S(1)} collective-permute-done((bf16[4,128,5,128]{1,3,2,0:T(8,128)(2,1)}, bf16[4,128,5,128]{1,3,2,0:T(8,128)(2,1)S(1)}, u32[]{:S(2)}, u32[]{:S(2)}) %collective-permute-start.7) | collective-permute-done | bytes 655392 | tf_op jit(solution)/shard_map/ppermute | solution.py:12
  443.4 2.0 convolution_bitcast_fusion
  445.5 5.0 copy.233
  450.4 5.7 %fusion.3 = bf16[4,2,128,5,128]{4,3,1,2,0:T(8,128)(2,1)S(1)} fusion(f32[4,128,5,2,128,1]{4,2,3,5,1,0:T(8,128)} %copy.233, f32[5,5,2,2,1,1]{0,1,3,2,5,4:T(8,128)S(1)} %copy.210), kind=kOutput, calls=%fused_computation.11 | convolution fusion | flops 79298560 | bytes 3932560 | tf_op jit(solution)/shard_map/wvts,aiwsk->ativk/dot_general | solution.py:58
  457.5 1.9 collective-permute-start.8
  460.4 11.4 %collective-permute-done.8 = bf16[4,128,5,128]{3,1,2,0:T(8,128)(2,1)} collective-permute-done((bf16[4,128,5,128]{3,1,2,0:T(8,128)(2,1)}, bf16[4,128,5,128]{3,1,2,0:T(8,128)(2,1)}, u32[]{:S(2)}, u32[]{:S(2)}) %collective-permute-start.8) | collective-permute-done | bytes 655392 | tf_op jit(solution)/shard_map/ppermute | solution.py:12
  471.9 1.4 copy.198
  476.2 46.9 %custom-call.18 = f32[4,128,128]{2,1,0:T(8,128)S(1)} custom-call(f32[4,128,128]{2,1,0:T(8,128)S(1)} %fusion.20), custom_call_target="Cholesky" | custom-call | tf_op jit(solution)/shard_map/jit(cholesky)/cholesky | solution.py:76
  523.4 39.3 %custom-call.19 = f32[4,1,128,128]{2,3,1,0:T(8,128)S(1)} custom-call(f32[4,1,128,128]{3,2,1,0:T(8,128)S(1)} %select_bitcast_fusion), custom_call_target="InvertDiagBlocksLowerTriangular" | custom-call | tf_op jit(solution)/shard_map/vmap(jit(_solve_triangular))/triangular_solve | solution.py:41
  563.8 1.7 fusion.4
  565.9 1.1 copy.207
  (85 shorter events, 23.0 us)
Async XLA Ops:
  0.6 45.8 %copy-start = (bf16[1,1,640,128]{3,2,1,0:T(8,128)(2,1)S(1)}, bf16[1,1,640,128]{3,2,1,0:T(8,128)(2,1)}, u32[]{:S(2)}) copy-start(bf16[1,1,640,128]{3,2,1,0:T(8,128)(2,1)} %param.12) | copy-start | bytes 491524
  0.6 14.7 %copy-start.1 = (bf16[4,128,5,128]{3,1,2,0:T(8,128)(2,1)S(1)}, bf16[4,128,5,128]{3,1,2,0:T(8,128)(2,1)}, u32[]{:S(2)}) copy-start(bf16[4,128,5,128]{3,1,2,0:T(8,128)(2,1)} %param.10) | copy-start | bytes 1966084
  2.0 12.1 %collective-permute-start = (bf16[4,128,2,128]{1,3,2,0:T(8,128)(2,1)S(1)}, bf16[4,128,2,128]{1,3,2,0:T(8,128)(2,1)S(1)}, u32[]{:S(2)}, u32[]{:S(2)}) collective-permute-start(bf16[4,128,2,128]{1,3,2,0:T(8,128)(2,1)S(1)} %bitcast_multiply_fusion), channel_id=1, source_target_pairs={{0,1},{1,2},{2,3},{3,4},{4,5},{5,6},{6,7},{7,8},{8,9},{9,10},{10,1... | collective-permute-start | bytes 786440 | tf_op jit(solution)/shard_map/ppermute | solution.py:23
  3.9 11.1 %collective-permute-start.1 = (bf16[4,128,2,128]{1,3,2,0:T(8,128)(2,1)S(1)}, bf16[4,128,2,128]{1,3,2,0:T(8,128)(2,1)S(1)}, u32[]{:S(2)}, u32[]{:S(2)}) collective-permute-start(bf16[4,128,2,128]{1,3,2,0:T(8,128)(2,1)S(1)} %bitcast_multiply_fusion), channel_id=1, source_target_pairs={{1,0},{2,1},{3,2},{4,3},{5,4},{6,5},{7,6},{8,7},{9,8},{10,9},{11,1... | collective-permute-start | bytes 786440 | tf_op jit(solution)/shard_map/ppermute | solution.py:25
  29.4 14.5 %collective-permute-start.2 = (bf16[4,128,5,128]{3,1,2,0:T(8,128)(2,1)}, bf16[4,128,5,128]{3,1,2,0:T(8,128)(2,1)}, u32[]{:S(2)}, u32[]{:S(2)}) collective-permute-start(bf16[4,128,5,128]{3,1,2,0:T(8,128)(2,1)} %copy.152), channel_id=1, source_target_pairs={{0,1},{1,2},{2,3},{3,4},{4,5},{5,6},{6,7},{7,8},{8,9},{9,10},{10,1... | collective-permute-start | bytes 1966088 | tf_op jit(solution)/shard_map/ppermute | solution.py:12
  32.2 14.3 %copy-start.9 = (f32[128]{0:T(128)}, f32[128]{0:T(128)S(1)}, u32[]{:S(2)}) copy-start(f32[128]{0:T(128)S(1)} %compare_convert_fusion) | copy-start | bytes 1540
  138.3 5.0 copy-start.4
  139.4 12.8 %collective-permute-start.3 = (bf16[4,128,5,128]{1,3,2,0:T(8,128)(2,1)}, bf16[4,128,5,128]{1,3,2,0:T(8,128)(2,1)}, u32[]{:S(2)}, u32[]{:S(2)}) collective-permute-start(bf16[4,128,5,128]{1,3,2,0:T(8,128)(2,1)} %bitcast.204), channel_id=1, source_target_pairs={{0,64},{64,128},{128,192},{1,65},{65,129},{129,193},{2,66},{66,130... | collective-permute-start | bytes 1966088 | tf_op jit(solution)/shard_map/ppermute | solution.py:12
  167.3 14.4 %collective-permute-start.4 = (bf16[4,128,5,128]{3,1,2,0:T(8,128)(2,1)}, bf16[4,128,5,128]{3,1,2,0:T(8,128)(2,1)}, u32[]{:S(2)}, u32[]{:S(2)}) collective-permute-start(bf16[4,128,5,128]{3,1,2,0:T(8,128)(2,1)} %copy.167), channel_id=1, source_target_pairs={{0,1},{1,2},{2,3},{3,4},{4,5},{5,6},{6,7},{7,8},{8,9},{9,10},{10,1... | collective-permute-start | bytes 1966088 | tf_op jit(solution)/shard_map/ppermute | solution.py:12
  170.5 13.7 %copy-start.10 = (f32[128]{0:T(128)S(1)}, f32[128]{0:T(128)}, u32[]{:S(2)}) copy-start(f32[128]{0:T(128)} %copy-done.9) | copy-start | bytes 1540
  277.5 22.9 %copy-start.2 = (bf16[4,128,256]{2,1,0:T(8,128)(2,1)}, bf16[4,128,256]{2,1,0:T(8,128)(2,1)S(1)}, u32[]{:S(2)}) copy-start(bf16[4,128,256]{2,1,0:T(8,128)(2,1)S(1)} %convolution_convert_fusion.6) | copy-start | bytes 786436
  282.2 16.1 %collective-permute-start.5 = (bf16[4,128,5,128]{1,3,2,0:T(8,128)(2,1)}, bf16[4,128,5,128]{1,3,2,0:T(8,128)(2,1)S(1)}, u32[]{:S(2)}, u32[]{:S(2)}) collective-permute-start(bf16[4,128,5,128]{1,3,2,0:T(8,128)(2,1)} %bitcast.205), channel_id=1, source_target_pairs={{0,64},{64,128},{128,192},{1,65},{65,129},{129,193},{2,66},{66,130... | collective-permute-start | bytes 1966088 | tf_op jit(solution)/shard_map/ppermute | solution.py:12
  312.4 14.3 %collective-permute-start.6 = (bf16[4,128,5,128]{3,1,2,0:T(8,128)(2,1)}, bf16[4,128,5,128]{3,1,2,0:T(8,128)(2,1)}, u32[]{:S(2)}, u32[]{:S(2)}) collective-permute-start(bf16[4,128,5,128]{3,1,2,0:T(8,128)(2,1)} %copy.182), channel_id=1, source_target_pairs={{0,1},{1,2},{2,3},{3,4},{4,5},{5,6},{6,7},{7,8},{8,9},{9,10},{10,1... | collective-permute-start | bytes 1966088 | tf_op jit(solution)/shard_map/ppermute | solution.py:12
  315.6 13.6 %copy-start.11 = (f32[128]{0:T(128)S(1)}, f32[128]{0:T(128)}, u32[]{:S(2)}) copy-start(f32[128]{0:T(128)} %copy-done.9) | copy-start | bytes 1540
  427.3 16.2 %collective-permute-start.7 = (bf16[4,128,5,128]{1,3,2,0:T(8,128)(2,1)}, bf16[4,128,5,128]{1,3,2,0:T(8,128)(2,1)S(1)}, u32[]{:S(2)}, u32[]{:S(2)}) collective-permute-start(bf16[4,128,5,128]{1,3,2,0:T(8,128)(2,1)} %bitcast.206), channel_id=1, source_target_pairs={{0,64},{64,128},{128,192},{1,65},{65,129},{129,193},{2,66},{66,130... | collective-permute-start | bytes 1966088 | tf_op jit(solution)/shard_map/ppermute | solution.py:12
  457.5 14.3 %collective-permute-start.8 = (bf16[4,128,5,128]{3,1,2,0:T(8,128)(2,1)}, bf16[4,128,5,128]{3,1,2,0:T(8,128)(2,1)}, u32[]{:S(2)}, u32[]{:S(2)}) collective-permute-start(bf16[4,128,5,128]{3,1,2,0:T(8,128)(2,1)} %copy.197), channel_id=1, source_target_pairs={{0,1},{1,2},{2,3},{3,4},{4,5},{5,6},{6,7},{7,8},{8,9},{9,10},{10,1... | collective-permute-start | bytes 1966088 | tf_op jit(solution)/shard_map/ppermute | solution.py:12
  460.1 14.3 %copy-start.12 = (f32[128]{0:T(128)S(1)}, f32[128]{0:T(128)}, u32[]{:S(2)}) copy-start(f32[128]{0:T(128)} %copy-done.9) | copy-start | bytes 1540
  460.4 14.5 %copy-start.6 = (bf16[4,128,640]{2,1,0:T(8,128)(2,1)}, bf16[4,128,640]{2,1,0:T(8,128)(2,1)S(1)}, u32[]{:S(2)}) copy-start(bf16[4,128,640]{2,1,0:T(8,128)(2,1)S(1)} %copy.199) | copy-start | bytes 1966084
  473.6 0.8 copy-start.8
  474.9 87.8 %copy-start.3 = (bf16[4,128,256]{2,1,0:T(8,128)(2,1)S(1)}, bf16[4,128,256]{2,1,0:T(8,128)(2,1)}, u32[]{:S(2)}) copy-start(bf16[4,128,256]{2,1,0:T(8,128)(2,1)} %copy-done.2) | copy-start | bytes 786436
  476.0 87.4 %copy-start.5 = (bf16[4,128,640]{2,1,0:T(8,128)(2,1)S(1)}, bf16[4,128,640]{2,1,0:T(8,128)(2,1)}, u32[]{:S(2)}) copy-start(bf16[4,128,640]{2,1,0:T(8,128)(2,1)} %copy-done.4) | copy-start | bytes 1966084
  562.7 1.1 copy-start.7
where the time goes:
time: 573 us; the launch traced here: 568 us
  other arithmetic  354 us (62%)
  waiting for transfers between devices  71.2 us (12%)
  local copies, waits for them, and re-layouts  58.1 us (10%)
  matrix products  55.3 us (10%)
  starting transfers between devices  28.1 us (5%)
    another operation x13, other arithmetic, site_step(): factor = jnp.linalg.cholesky(gram_matrix)  190 us
    another operation x9, other arithmetic, solve_lower(): return jax.scipy.linalg.solve_triangular(factor, right_side.T, lower=True)  159 us
    ppermute x7, waiting for transfers between devices, from_behind(): return lax.ppermute(x, axis, pairs)  70.4 us
    dot_general x4, matrix products, site_step(): jnp.einsum('wvts,aiwsk->ativk', coupled, products, precision=lax.Precisio...  22.9 us
    transpose x4, local copies, waits for them, and re-layouts, site_step(): jnp.einsum('aiwj,awjsk->aiwsk', carried, selected, preferred_element_type...  19.9 us
    ppermute x7, starting transfers between devices, from_behind(): return lax.ppermute(x, axis, pairs)  19 us
  transfers between devices with their start and end apart: 9, of which 8 were waited for; matrix products, arithmetic and copies ran while one was open for 3% of the time, Pallas kernels for 0%

commit v1 on v0

v1 whole, which is shorter than its diff:
```python
import functools

import jax
import jax.numpy as jnp
from jax import lax
from jax.experimental import pallas as pl
from jax.experimental.pallas import tpu as pltpu
from jax.sharding import PartitionSpec as P

CHARGES = (0, 1, -1, 0, 0)
WB = len(CHARGES)
DS = 128
ROWS = 8
MESH = pl.DeviceIdType.MESH
F32 = jnp.float32
BF16 = jnp.bfloat16
NN = (((1,), (0,)), ((), ()))
NT = (((1,), (1,)), ((), ()))


def dot(a, b, dims=NN):
    return lax.dot_general(a, b, dims, preferred_element_type=F32)


def halves(x):
    high = x.astype(BF16)
    return high, (x - high.astype(F32)).astype(BF16)


def wide(v, width):
    return v if width == v.shape[1] else jnp.concatenate([v] * (width // v.shape[1]), axis=1)


def invert_factor(work, inverse):
    width = work.shape[1]

    def block(step, carry):
        first = pl.multiple_of(step * ROWS, ROWS)
        shift = lax.rem(DS - first, DS)
        rows = work[pl.ds(first, ROWS), :]
        turned = pltpu.roll(work[:, :DS], shift, axis=1)
        corner = pltpu.roll(rows[:, :DS], shift, axis=1)
        columns = [jnp.broadcast_to(turned[:, c : c + 1], (DS, DS)) for c in range(ROWS)]
        tops = [jnp.broadcast_to(corner[:, c : c + 1], (ROWS, DS)) for c in range(ROWS)]
        low = [
            [jnp.broadcast_to(tops[c][r : r + 1, :], (ROWS, DS)) if r >= c else None for c in range(ROWS)]
            for r in range(ROWS)
        ]
        scale = []
        for c in range(ROWS):
            scale.append(lax.rsqrt(low[c][c]))
            for r in range(c + 1, ROWS):
                low[r][c] = low[r][c] * scale[c]
            for q in range(c + 1, ROWS):
                for r in range(q, ROWS):
                    low[r][q] = low[r][q] - low[r][c] * low[q][c]
        upper = []
        for c in range(ROWS):
            x = jnp.broadcast_to(rows[c : c + 1, :], (ROWS, width))
            for q in range(c):
                x = x - wide(low[c][q], width) * upper[q]
            upper.append(x * wide(scale[c], width))
        inverse[pl.ds(first, ROWS), :] = jnp.concatenate([u[0:1, DS:] for u in upper], axis=0)
        solved = [None] * ROWS
        for c in reversed(range(ROWS)):
            x = upper[c]
            for q in range(c + 1, ROWS):
                x = x - wide(low[q][c], width) * solved[q]
            solved[c] = x * wide(scale[c], width)
        for i in range(DS // ROWS):
            part = pl.ds(i * ROWS, ROWS)
            rest = work[part, :]
            for c in range(ROWS):
                rest = rest - wide(columns[c][i * ROWS : (i + 1) * ROWS, :], width) * solved[c]
            work[part, :] = rest
        return carry

    lax.fori_loop(0, DS // ROWS, block, 0)


def kernel(
    sites, sectors,
    mpo, ranks, blocks_in, carry_in, sketch_in,
    sites_out, carry_out,
    blk, sk, car, terms, sent, below, y_out, y_in, iso, coupled, sketched, plain, work, inverse,
    first_sem, blk_sem, sk_sem, pass_sem, load_sem, y_send, y_recv, t_send, t_recv, o_send, o_recv,
):
    c = lax.axis_index("chain")
    p = lax.axis_index("block")
    up = {"block": lax.rem(p + 1, sectors)}
    down = {"block": lax.rem(p + sectors - 1, sectors)}

    def remote(src, dst, send, recv, to):
        return pltpu.make_async_remote_copy(
            src_ref=src, dst_ref=dst, send_sem=send, recv_sem=recv, device_id=to, device_id_type=MESH
        )

    local_carry = pltpu.make_async_copy(carry_in.at[c], car.at[0], load_sem)
    local_block = pltpu.make_async_copy(blocks_in.at[c], blk.at[c, 0], blk_sem.at[c, 0])
    local_sketch = pltpu.make_async_copy(sketch_in, sk.at[c, 0], sk_sem.at[c, 0])
    local_block.start()
    local_sketch.start()
    local_carry.start()

    barrier = pltpu.get_barrier_semaphore()
    for d in range(1, sites):
        pl.semaphore_signal(barrier, inc=1, device_id={"chain": lax.rem(c + d, sites)}, device_id_type=MESH)
    pl.semaphore_signal(barrier, inc=1, device_id=up, device_id_type=MESH)
    pl.semaphore_signal(barrier, inc=1, device_id=down, device_id_type=MESH)
    pl.semaphore_wait(barrier, sites + 1)

    def share(d, which):
        peer = lax.rem(c + d, sites)
        to = {"chain": peer}
        if which == 0:
            return remote(blocks_in.at[peer], blk.at[c, 0], first_sem.at[0, d], blk_sem.at[c, 0], to)
        return remote(sketch_in, sk.at[c, 0], first_sem.at[1, d], sk_sem.at[c, 0], to)

    def send_shares():
        for which in range(2):
            for d in range(1, sites):
                share(d, which).start()

    def passed(k, which):
        if which == 0:
            return remote(blk.at[k, 0], blk.at[k, 1], pass_sem.at[k, 0], blk_sem.at[k, 1], up)
        if which == 1:
            return remote(blk.at[k, 0], blk.at[k, 2], pass_sem.at[k, 1], blk_sem.at[k, 2], down)
        return remote(sk.at[k, 0], sk.at[k, 1], pass_sem.at[k, 2], sk_sem.at[k, 1], down)

    def pass_on(k):
        pltpu.make_async_copy(blk.at[k, 0], blk.at[k, 0], blk_sem.at[k, 0]).wait()
        passed(k, 0).start()
        passed(k, 1).start()
        pltpu.make_async_copy(sk.at[k, 0], sk.at[k, 0], sk_sem.at[k, 0]).wait()
        passed(k, 2).start()

    top = (p < sectors - 1).astype(F32)
    below_top = (p < sectors - 2).astype(F32)
    bottom = (p > 0).astype(F32)

    def prepare(k):
        passed(k, 0).wait_recv()
        passed(k, 1).wait_recv()
        for w in range(WB):
            where = {0: 0, 1: 1, -1: 2}[CHARGES[w]]
            if w < 3:
                plain[...] = blk[k, where].astype(F32)
                own = [plain[pl.ds(s, DS, stride=2), :] for s in range(2)]
                if w == 0:
                    centre = own
            else:
                own = centre
            for v in range(WB):
                for t in range(2):
                    s = t - CHARGES[v] + CHARGES[w]
                    if s not in (0, 1):
                        continue
                    weight = mpo[k, w, t, s, v]
                    if where == 0 and s == 1:
                        weight = weight * top
                    elif where == 1:
                        weight = weight * bottom
                    elif where == 2:
                        weight = weight * (top if s == 0 else below_top)
                    coupled[t, pl.ds(w * DS, DS), pl.ds(v * DS, DS)] = (own[s] * weight).astype(BF16)
        passed(k, 2).wait_recv()
        for t in range(2):
            product = dot(coupled[t], sk[k, t])
            for w in range(WB):
                sketched[pl.ds(t * DS, DS), pl.ds(w * DS, DS)] = product[w * DS : (w + 1) * DS, :].T.astype(BF16)

    @pl.when(c == 0)
    def _():
        send_shares()

    coupled[...] = jnp.zeros_like(coupled)
    pass_on(0)

    @pl.when(c > 0)
    def _():
        send_shares()

    prepare(0)
    local_carry.wait()

    def output(k, which):
        return (iso.at[k], sites_out.at[c]) if which == 0 else (car.at[k + 1], carry_out.at[c])

    def outgoing(k, which):
        return remote(*output(k, which), o_send.at[k, which], o_recv.at[c, which], {"chain": k})

    def kept(k, which):
        return pltpu.make_async_copy(*output(k, which), o_send.at[k, which])

    def deliver(k, which):
        @pl.when(c == k)
        def _():
            kept(k, which).start()

        @pl.when(c != k)
        def _():
            outgoing(k, which).start()

    row_ids = lax.broadcasted_iota(jnp.int32, (DS, DS), 0)
    column_ids = lax.broadcasted_iota(jnp.int32, (DS, DS), 1)

    def step(k, carry):
        carried = jnp.concatenate([car[k, w] for w in range(WB)], axis=1)
        y = dot(sketched[...], carried, NT)
        y_out[k] = y[DS:]
        y_copy = remote(y_out.at[k], y_in.at[k], y_send.at[k], y_recv.at[k], up)
        y_copy.start()
        sent[k] = dot(carried, coupled[1]).astype(BF16)
        t_copy = remote(sent.at[k], below.at[k], t_send.at[k], t_recv.at[k], up)
        t_copy.start()
        terms[...] = dot(carried, coupled[0]).astype(BF16)

        @pl.when(k + 1 < sites)
        def _():
            pass_on(k + 1)

        rank = ranks[0, k]
        upper_rank = jnp.where(p > 0, rank, 0)
        y_copy.wait_recv()
        y0 = jnp.where(row_ids < rank, y[:DS], 0.0)
        y1 = jnp.where(row_ids < upper_rank, y_in[k], 0.0)
        high, low = halves(jnp.concatenate([y0, y1], axis=1))
        gram = dot(
            jnp.concatenate([high, high, low], axis=1), jnp.concatenate([high, low, high], axis=1), NT
        )
        ridge = jnp.where(row_ids < rank, DS / 4.0, 1.0)
        work[:, :DS] = gram + jnp.where(row_ids == column_ids, ridge, 0.0)
        work[:, DS:] = jnp.where(row_ids == column_ids, 1.0, 0.0)
        invert_factor(work, inverse)
        inv_high, inv_low = halves(inverse[...])
        frame = dot(
            jnp.concatenate([inv_high, inv_low, inv_high], axis=1),
            jnp.concatenate([high, high, low], axis=0),
        )
        plain[pl.ds(0, DS, stride=2), :] = frame[:, :DS]
        plain[pl.ds(1, DS, stride=2), :] = frame[:, DS:]
        iso[k] = plain[...].astype(BF16)
        deliver(k, 0)
        t_copy.wait_recv()
        new = dot(frame.astype(BF16), jnp.concatenate([terms[...], below[k]], axis=0)).astype(BF16)
        for v in range(WB):
            car[k + 1, v] = new[:, v * DS : (v + 1) * DS]
        deliver(k, 1)

        @pl.when(k + 1 < sites)
        def _():
            prepare(k + 1)

        y_copy.wait_send()
        t_copy.wait_send()
        return carry

    lax.fori_loop(0, sites, step, 0)

    for d in range(1, sites):
        for which in range(2):
            share(d, which).wait_send()
    for k in range(sites):
        for which in range(3):
            passed(k, which).wait_send()

        @pl.when(c == k)
        def _():
            for which in range(2):
                kept(k, which).wait()

        @pl.when(c != k)
        def _():
            for which in range(2):
                outgoing(k, which).wait_send()

    for d in range(1, sites):
        peer = lax.rem(c + d, sites)
        remote(iso.at[0], sites_out.at[peer], o_send.at[0, 0], o_recv.at[peer, 0], {"chain": peer}).wait_recv()
        remote(car.at[1], carry_out.at[peer], o_send.at[0, 1], o_recv.at[peer, 1], {"chain": peer}).wait_recv()


def per_device(site_blocks, left_carry, mpo, sketch, ranks):
    sites = lax.axis_size("chain")
    sectors = lax.axis_size("block")
    states = left_carry.shape[0]
    dma = pltpu.SemaphoreType.DMA
    vmem = pltpu.VMEM
    new_sites, carries = pl.pallas_call(
        functools.partial(kernel, sites, sectors),
        name="zip_up",
        out_shape=(
            jax.ShapeDtypeStruct((states, 2 * DS, DS), BF16),
            jax.ShapeDtypeStruct((states, WB, DS, DS), BF16),
        ),
        in_specs=[
            pl.BlockSpec(memory_space=pltpu.SMEM),
            pl.BlockSpec(memory_space=pltpu.SMEM),
            pl.BlockSpec(memory_space=pl.ANY),
            pl.BlockSpec(memory_space=pl.ANY),
            pl.BlockSpec(memory_space=pl.ANY),
        ],
        out_specs=(pl.BlockSpec(memory_space=pl.ANY), pl.BlockSpec(memory_space=pl.ANY)),
        scratch_shapes=[
            vmem((sites, 3, 2 * DS, DS), BF16),
            vmem((sites, 2, WB * DS, DS), BF16),
            vmem((sites + 1, WB, DS, DS), BF16),
            vmem((DS, WB * DS), BF16),
            vmem((sites, DS, WB * DS), BF16),
            vmem((sites, DS, WB * DS), BF16),
            vmem((sites, DS, DS), F32),
            vmem((sites, DS, DS), F32),
            vmem((sites, 2 * DS, DS), BF16),
            vmem((2, WB * DS, WB * DS), BF16),
            vmem((2 * DS, WB * DS), BF16),
            vmem((2 * DS, DS), F32),
            vmem((DS, 2 * DS), F32),
            vmem((DS, DS), F32),
            dma((2, sites)),
            dma((sites, 3)),
            dma((sites, 2)),
            dma((sites, 3)),
            dma,
            dma((sites,)),
            dma((sites,)),
            dma((sites,)),
            dma((sites,)),
            dma((sites, 2)),
            dma((sites, 2)),
        ],
        compiler_params=pltpu.CompilerParams(
            collective_id=0, has_side_effects=True, vmem_limit_bytes=40 * 2**20
        ),
    )(
        jnp.transpose(mpo, (0, 1, 3, 4, 2)),
        jnp.transpose(ranks),
        site_blocks.reshape(states, 2 * DS, DS),
        jnp.transpose(left_carry, (0, 2, 1, 3)),
        sketch.reshape(WB * DS, DS),
    )
    return (
        new_sites.reshape(1, states, DS, 2, DS),
        jnp.transpose(carries, (0, 2, 1, 3))[None],
    )


def solution(mesh):
    return jax.shard_map(
        per_device,
        mesh=mesh,
        in_specs=(
            P("chain", None, "block", None, None),
            P(None, "block", None, None),
            P(),
            P("chain", "block", None, None),
            P(None, "block"),
        ),
        out_specs=(P("chain", None, "block", None, None), P("chain", None, "block", None, None)),
        check_vma=False,
    )
```

time: 573 us -> 87.6 us (0.15)
  the two profiles are of different devices: /device:TPU:12 before, /device:TPU:24 now
where the time goes in v1:
time: 87.6 us; the launch traced here: 86.9 us
  Pallas kernels  80.4 us (92%)
  local copies, waits for them, and re-layouts  5.92 us (7%)
    pallas_call x1, Pallas kernels, per_device(): pl.pallas_call(functools.partial(kernel, sites, sectors), name='zip_up',...  80.4 us
    unnamed x12, local copies, waits for them, and re-layouts  5.92 us

profile of v1, /device:TPU:24, one launch (start us, length us, event | category | flops | bytes accessed | tf_op | source)
XLA Modules:
  0.0 86.9 jit_solution(15372921941241106635)
XLA Ops:
  0.6 0.0 copy-start.4
  0.6 0.6 copy-done.4
  1.3 0.0 copy-start
  1.3 1.1 %copy-done = bf16[4,128,5,128]{3,1,2,0:T(8,128)(2,1)S(1)} copy-done((bf16[4,128,5,128]{3,1,2,0:T(8,128)(2,1)S(1)}, bf16[4,128,5,128]{3,1,2,0:T(8,128)(2,1)}, u32[]{:S(2)}) %copy-start) | copy-done | bytes 655384
  2.4 0.0 copy-start.1
  2.4 0.9 %copy-done.1 = bf16[1,4,128,2,128]{4,3,2,1,0:T(2,128)(2,1)S(1)} copy-done((bf16[1,4,128,2,128]{4,3,2,1,0:T(2,128)(2,1)S(1)}, bf16[1,4,128,2,128]{4,3,2,1,0:T(2,128)(2,1)}, u32[]{:S(2)}) %copy-start.1) | copy-done | bytes 262168
  3.3 0.0 copy-start.2
  3.3 0.9 %copy-done.2 = bf16[1,1,640,128]{3,2,1,0:T(8,128)(2,1)S(1)} copy-done((bf16[1,1,640,128]{3,2,1,0:T(8,128)(2,1)S(1)}, bf16[1,1,640,128]{3,2,1,0:T(8,128)(2,1)}, u32[]{:S(2)}) %copy-start.2) | copy-done | bytes 163864
  4.2 0.0 copy-start.3
  4.2 0.8 copy-done.3
  5.0 80.4 %zip_up.1 = (bf16[4,256,128]{2,1,0:T(8,128)(2,1)S(1)}, bf16[4,5,128,128]{3,2,1,0:T(8,128)(2,1)S(1)}) custom-call(f32[4,5,2,2,5]{4,3,2,1,0:T(2,128)S(1)} %bitcast.14, s32[1,4]{1,0:T(1,128)S(1)} %bitcast.15, bf16[4,256,128]{2,1,0:T(8,128)(2,1)S(1)} %bitcast.12, bf16[4,5,128,128]{3,2,1,0:T(8,128)(2,1)S(1)} %bitcast.10, bf16[640,128]{1,0:T(8,128)(2,1)S(1)} %bitcast.13), custom_call_target="tpu_custom_call" | custom-call | tf_op jit(solution)/shard_map/zip_up/pallas_call | solution.py:290
  85.4 0.7 copy.9
  86.1 0.8 copy.10
Async XLA Ops:
  0.6 0.7 copy-start.4
  1.3 1.1 %copy-start = (bf16[4,128,5,128]{3,1,2,0:T(8,128)(2,1)S(1)}, bf16[4,128,5,128]{3,1,2,0:T(8,128)(2,1)}, u32[]{:S(2)}) copy-start(bf16[4,128,5,128]{3,1,2,0:T(8,128)(2,1)} %param.6) | copy-start | bytes 1966084
  2.4 0.9 %copy-start.1 = (bf16[1,4,128,2,128]{4,3,2,1,0:T(2,128)(2,1)S(1)}, bf16[1,4,128,2,128]{4,3,2,1,0:T(2,128)(2,1)}, u32[]{:S(2)}) copy-start(bf16[1,4,128,2,128]{4,3,2,1,0:T(2,128)(2,1)} %param.5) | copy-start | bytes 786436
  3.3 0.9 %copy-start.2 = (bf16[1,1,640,128]{3,2,1,0:T(8,128)(2,1)S(1)}, bf16[1,1,640,128]{3,2,1,0:T(8,128)(2,1)}, u32[]{:S(2)}) copy-start(bf16[1,1,640,128]{3,2,1,0:T(8,128)(2,1)} %param.8) | copy-start | bytes 491524
  4.2 0.8 copy-start.3

commit v2 on v1

v2 whole, which is shorter than its diff:
```python
import functools

import jax
import jax.numpy as jnp
from jax import lax
from jax.experimental import pallas as pl
from jax.experimental.pallas import tpu as pltpu
from jax.sharding import PartitionSpec as P

CHARGES = (0, 1, -1, 0, 0)
WB = len(CHARGES)
DS = 128
ROWS = 8
MESH = pl.DeviceIdType.MESH
F32 = jnp.float32
BF16 = jnp.bfloat16
NN = (((1,), (0,)), ((), ()))
NT = (((1,), (1,)), ((), ()))


def dot(a, b, dims=NN):
    return lax.dot_general(a, b, dims, preferred_element_type=F32)


def halves(x):
    high = x.astype(BF16)
    return high, (x - high.astype(F32)).astype(BF16)


def wide(v, width):
    return v if width == v.shape[1] else jnp.concatenate([v] * (width // v.shape[1]), axis=1)


def invert_factor(work, inverse):
    width = work.shape[1]
    count = DS // ROWS
    part = [slice(i * ROWS, (i + 1) * ROWS) for i in range(count)]

    def lanes(x, first):
        return [jnp.broadcast_to(x[:, first + q : first + q + 1], (ROWS, DS)) for q in range(ROWS)]

    def entry(columns, r, q):
        return jnp.broadcast_to(columns[q][r : r + 1, :], (ROWS, DS))

    rows = work[part[0], :]
    corner = lanes(rows, 0)
    for block in range(count):
        first = block * ROWS
        low = [[entry(corner, r, q) if r >= q else None for q in range(ROWS)] for r in range(ROWS)]
        scale = []
        for q in range(0, ROWS, 2):
            e = q + 1
            inv = lax.rsqrt(low[q][q])
            det = low[q][q] * low[e][e] - low[e][q] * low[e][q]
            inv_e = lax.rsqrt(det) * (low[q][q] * inv)
            scale += [inv, inv_e]
            for r in range(e, ROWS):
                low[r][q] = low[r][q] * inv
            for r in range(e + 1, ROWS):
                low[r][e] = (low[r][e] - low[r][q] * low[e][q]) * inv_e
            for n in range(e + 1, ROWS):
                for r in range(n, ROWS):
                    low[r][n] = low[r][n] - (low[r][q] * low[n][q] + low[r][e] * low[n][e])
        upper = []
        for q in range(ROWS):
            x = jnp.broadcast_to(rows[q : q + 1, :], (ROWS, width))
            for n in range(q):
                x = x - wide(low[q][n], width) * upper[n]
            upper.append(x * wide(scale[q], width))
        for q in range(ROWS):
            inverse[first + q : first + q + 1, :] = upper[q][0:1, DS:]
        if block + 1 == count:
            break
        below = work[part[block + 1], :]
        left = []
        for q, x in enumerate(lanes(below, first)):
            for n in range(q):
                x = x - left[n] * low[q][n]
            left.append(x * scale[q])
        corner = lanes(below, first + ROWS)
        for q in range(ROWS):
            for n in range(ROWS):
                corner[q] = corner[q] - left[n] * jnp.broadcast_to(left[n][q : q + 1, :], (ROWS, DS))
        rows = below
        for q in range(ROWS):
            rows = rows - wide(left[q], width) * upper[q]
        solved = [None] * ROWS
        for q in reversed(range(ROWS)):
            x = upper[q]
            for n in range(q + 1, ROWS):
                x = x - wide(low[n][q], width) * solved[n]
            solved[q] = x * wide(scale[q], width)
        for i in range(block + 2, count):
            rest = work[part[i], :]
            columns = lanes(rest, first)
            for q in range(ROWS):
                rest = rest - wide(columns[q], width) * solved[q]
            work[part[i], :] = rest


def kernel(
    sites, sectors,
    mpo_in, ranks_in, blocks_in, carry_in, sketch_in,
    sites_out, carry_out,
    mpo, ranks, blk, sk, car, sent, below, iso, coupled, plain, work, inverse,
    share_sem, blk_sem, sk_sem, pass_sem, load_sem, t_send, t_recv, o_send, o_recv,
):
    c = lax.axis_index("chain")
    p = lax.axis_index("block")
    up = {"block": lax.rem(p + 1, sectors)}
    down = {"block": lax.rem(p + sectors - 1, sectors)}

    def remote(src, dst, send, recv, to):
        return pltpu.make_async_remote_copy(
            src_ref=src, dst_ref=dst, send_sem=send, recv_sem=recv, device_id=to, device_id_type=MESH
        )

    loads = (
        pltpu.make_async_copy(mpo_in, mpo, load_sem.at[0]),
        pltpu.make_async_copy(ranks_in, ranks, load_sem.at[1]),
        pltpu.make_async_copy(carry_in.at[c], car.at[0], load_sem.at[2]),
    )
    pltpu.make_async_copy(blocks_in.at[c], blk.at[c, 0], blk_sem.at[c, 0]).start()
    pltpu.make_async_copy(sketch_in, sk.at[c], sk_sem.at[c]).start()
    for load in loads:
        load.start()

    barrier = pltpu.get_barrier_semaphore()
    for d in range(1, sites):
        pl.semaphore_signal(barrier, inc=1, device_id={"chain": lax.rem(c + d, sites)}, device_id_type=MESH)
    pl.semaphore_signal(barrier, inc=1, device_id=up, device_id_type=MESH)
    pl.semaphore_signal(barrier, inc=1, device_id=down, device_id_type=MESH)
    pl.semaphore_wait(barrier, sites + 1)

    def share(d, which):
        peer = lax.rem(c + d, sites)
        to = {"chain": peer}
        if which == 0:
            return remote(blocks_in.at[peer], blk.at[c, 0], share_sem.at[0, d], blk_sem.at[c, 0], to)
        return remote(sketch_in, sk.at[c], share_sem.at[1, d], sk_sem.at[c], to)

    def passed(k, which, src):
        to = up if which == 0 else down
        return remote(src, blk.at[k, which + 1], pass_sem.at[k, which], blk_sem.at[k, which + 1], to)

    ORDER = (1, sites - 1) + tuple(range(2, sites - 1))

    def share_blocks():
        for d in ORDER:
            share(d, 0).start()
        for which in range(2):
            passed(c, which, blocks_in.at[c]).start()

    def share_sketch():
        for d in ORDER:
            share(d, 1).start()

    def arrived(ref, sem):
        pltpu.make_async_copy(ref, ref, sem).wait()

    def pass_on(k):
        arrived(blk.at[k, 0], blk_sem.at[k, 0])

        @pl.when(c != k)
        def _():
            for which in range(2):
                passed(k, which, blk.at[k, 0]).start()

    top = (p < sectors - 1).astype(F32)
    below_top = (p < sectors - 2).astype(F32)
    bottom = (p > 0).astype(F32)

    def prepare(k):
        for w in range(WB):
            where = {0: 0, 1: 1, -1: 2}[CHARGES[w]]
            if w < 3:
                if where:
                    arrived(blk.at[k, where], blk_sem.at[k, where])
                plain[w] = blk[k, where].astype(F32)
            own = [plain[where, pl.ds(s, DS, stride=2), :] for s in range(2)]
            for v in range(WB):
                for t in range(2):
                    s = t - CHARGES[v] + CHARGES[w]
                    if s not in (0, 1):
                        continue
                    weight = mpo[k, w, t, s : s + 1, v : v + 1]
                    if where == 0 and s == 1:
                        weight = weight * top
                    elif where == 1:
                        weight = weight * bottom
                    elif where == 2:
                        weight = weight * (top if s == 0 else below_top)
                    coupled[t, pl.ds(w * DS, DS), pl.ds(v * DS, DS)] = (own[s] * weight).astype(BF16)

    share_blocks()

    @pl.when(c == 0)
    def _():
        share_sketch()

    for t in range(2):
        for w in range(WB):
            for v in range(WB):
                if t - CHARGES[v] + CHARGES[w] not in (0, 1):
                    coupled[t, pl.ds(w * DS, DS), pl.ds(v * DS, DS)] = jnp.zeros((DS, DS), BF16)
    for load in loads:
        load.wait()
    pass_on(0)
    prepare(0)

    def output(k, which):
        return (iso.at[k], sites_out.at[c]) if which == 0 else (car.at[k + 1], carry_out.at[c])

    def outgoing(k, which):
        return remote(*output(k, which), o_send.at[k, which], o_recv.at[c, which], {"chain": k})

    def kept(k, which):
        return pltpu.make_async_copy(*output(k, which), o_send.at[k, which])

    def deliver(k, which):
        @pl.when(c == k)
        def _():
            kept(k, which).start()

        @pl.when(c != k)
        def _():
            outgoing(k, which).start()

    row_ids = lax.broadcasted_iota(jnp.int32, (DS, DS), 0)
    column_ids = lax.broadcasted_iota(jnp.int32, (DS, DS), 1)
    rows_f = row_ids.astype(F32)
    site_ids = lax.broadcasted_iota(jnp.int32, (1, sites), 1)
    CUTS = ((0, 3), (3, WB))

    def raised(k, part):
        v0, v1 = CUTS[part]
        cut = pl.ds(v0, v1 - v0)
        return remote(sent.at[k, cut], below.at[k, cut], t_send.at[k, part], t_recv.at[k, part], up)

    def step(k, carry):
        carried = jnp.concatenate([car[k, w] for w in range(WB)], axis=1)
        for part, (v0, v1) in enumerate(CUTS):
            rows = dot(carried, coupled[1, :, pl.ds(v0 * DS, (v1 - v0) * DS)]).astype(BF16)
            for v in range(v0, v1):
                sent[k, v] = rows[:, (v - v0) * DS : (v - v0 + 1) * DS]
            raised(k, part).start()
        terms = dot(carried, coupled[0]).astype(BF16)
        arrived(sk.at[k], sk_sem.at[k])
        tests = sk[k].T
        rank = jnp.sum(jnp.where(site_ids == k, ranks[...].astype(F32), 0.0), axis=1, keepdims=True)
        upper_rank = rank * bottom
        y0 = jnp.where(rows_f < rank, dot(tests, terms, NT), 0.0)

        @pl.when(k == 0)
        def _():
            for later in range(1, sites):
                pass_on(later)

        @pl.when(jnp.logical_and(k == 0, c > 0))
        def _():
            share_sketch()

        for part in range(len(CUTS)):
            raised(k, part).wait_recv()
        lower = jnp.concatenate([below[k, v] for v in range(WB)], axis=1)
        y1 = jnp.where(rows_f < upper_rank, dot(tests, lower, NT), 0.0)
        high, low = halves(jnp.concatenate([y0, y1], axis=1))
        gram = dot(
            jnp.concatenate([high, high, low], axis=1), jnp.concatenate([high, low, high], axis=1), NT
        )
        ridge = jnp.where(rows_f < rank, DS / 4.0, 1.0)
        work[:, :DS] = gram + jnp.where(row_ids == column_ids, ridge, 0.0)
        work[:, DS:] = jnp.where(row_ids == column_ids, 1.0, 0.0)
        invert_factor(work, inverse)

        inv_high, inv_low = halves(inverse[...])
        frame = dot(
            jnp.concatenate([inv_high, inv_low, inv_high], axis=1),
            jnp.concatenate([high, high, low], axis=0),
        )
        new = dot(frame.astype(BF16), jnp.concatenate([terms, lower], axis=0)).astype(BF16)
        for v in range(WB):
            car[k + 1, v] = new[:, v * DS : (v + 1) * DS]
        deliver(k, 1)
        plain[0, pl.ds(0, DS, stride=2), :] = frame[:, :DS]
        plain[0, pl.ds(1, DS, stride=2), :] = frame[:, DS:]
        iso[k] = plain[0].astype(BF16)
        deliver(k, 0)

        @pl.when(k + 1 < sites)
        def _():
            prepare(k + 1)

        return carry

    lax.fori_loop(0, sites, step, 0)

    for d in range(1, sites):
        for which in range(2):
            share(d, which).wait_send()
    for k in range(sites):
        for part in range(2):
            passed(k, part, blk.at[k, 0]).wait_send()
            raised(k, part).wait_send()

        @pl.when(c == k)
        def _():
            for which in range(2):
                kept(k, which).wait()

        @pl.when(c != k)
        def _():
            for which in range(2):
                outgoing(k, which).wait_send()

    for d in range(1, sites):
        peer = lax.rem(c + d, sites)
        remote(iso.at[0], sites_out.at[peer], o_send.at[0, 0], o_recv.at[peer, 0], {"chain": peer}).wait_recv()
        remote(car.at[1], carry_out.at[peer], o_send.at[0, 1], o_recv.at[peer, 1], {"chain": peer}).wait_recv()


def per_device(site_blocks, left_carry, mpo, sketch, ranks):
    sites = lax.axis_size("chain")
    sectors = lax.axis_size("block")
    states = left_carry.shape[0]
    dma = pltpu.SemaphoreType.DMA
    vmem = pltpu.VMEM
    new_sites, carries = pl.pallas_call(
        functools.partial(kernel, sites, sectors),
        name="zip_up",
        out_shape=(
            jax.ShapeDtypeStruct((states, 2 * DS, DS), BF16),
            jax.ShapeDtypeStruct((states, WB, DS, DS), BF16),
        ),
        in_specs=[
            pl.BlockSpec(memory_space=pltpu.HBM),
            pl.BlockSpec(memory_space=pltpu.HBM),
            pl.BlockSpec(memory_space=pltpu.HBM),
            pl.BlockSpec(memory_space=pltpu.HBM),
            pl.BlockSpec(memory_space=pltpu.HBM),
        ],
        out_specs=(pl.BlockSpec(memory_space=pltpu.HBM), pl.BlockSpec(memory_space=pltpu.HBM)),
        scratch_shapes=[
            vmem(mpo.shape[:2] + (2, 2, WB), F32),
            vmem((1, sites), jnp.int32),
            vmem((sites, 3, 2 * DS, DS), BF16),
            vmem((sites, WB * DS, DS), BF16),
            vmem((sites + 1, WB, DS, DS), BF16),
            vmem((sites, WB, DS, DS), BF16),
            vmem((sites, WB, DS, DS), BF16),
            vmem((sites, 2 * DS, DS), BF16),
            vmem((2, WB * DS, WB * DS), BF16),
            vmem((3, 2 * DS, DS), F32),
            vmem((DS, 2 * DS), F32),
            vmem((DS, DS), F32),
            dma((2, sites)),
            dma((sites, 3)),
            dma((sites,)),
            dma((sites, 2)),
            dma((3,)),
            dma((sites, 2)),
            dma((sites, 2)),
            dma((sites, 2)),
            dma((sites, 2)),
        ],
        compiler_params=pltpu.CompilerParams(
            collective_id=0, has_side_effects=True, vmem_limit_bytes=60 * 2**20
        ),
    )(
        jnp.transpose(mpo, (0, 1, 3, 4, 2)),
        jnp.transpose(ranks),
        site_blocks.reshape(states, 2 * DS, DS),
        jnp.transpose(left_carry, (0, 2, 1, 3)),
        sketch.reshape(WB * DS, DS),
    )
    return (
        new_sites.reshape(1, states, DS, 2, DS),
        jnp.transpose(carries, (0, 2, 1, 3))[None],
    )


def solution(mesh):
    return jax.shard_map(
        per_device,
        mesh=mesh,
        in_specs=(
            P("chain", None, "block", None, None),
            P(None, "block", None, None),
            P(),
            P("chain", "block", None, None),
            P(None, "block"),
        ),
        out_specs=(P("chain", None, "block", None, None), P("chain", None, "block", None, None)),
        check_vma=False,
    )
```

time: 87.6 us -> 57.9 us (0.66)
  Pallas kernels: 80.4 us -> 53.2 us
  local copies, waits for them, and re-layouts: 5.92 us -> 3.82 us
    pallas_call x1, Pallas kernels: 80.4 us -> 53.2 us  [per_device(): pl.pallas_call(functools.partial(kernel, sites, sectors), name='zip_up',...]
    unnamed x12 -> x2, local copies, waits for them, and re-layouts: 5.92 us -> 3.82 us
where the time goes in v2:
time: 57.9 us; the launch traced here: 57.7 us
  Pallas kernels  53.2 us (92%)
  local copies, waits for them, and re-layouts  3.82 us (7%)
  between operations  0.64 us (1%)
    pallas_call x1, Pallas kernels, per_device(): pl.pallas_call(functools.partial(kernel, sites, sectors), name='zip_up',...  53.2 us
    unnamed x2, local copies, waits for them, and re-layouts  3.82 us

profile of v2, /device:TPU:24, one launch (start us, length us, event | category | flops | bytes accessed | tf_op | source)
XLA Modules:
  0.0 57.7 jit_solution(15572967689885507838)
XLA Ops:
  0.6 53.2 %zip_up.1 = (bf16[4,256,128]{2,1,0:T(8,128)(2,1)}, bf16[4,5,128,128]{3,2,1,0:T(8,128)(2,1)}) custom-call(f32[4,5,2,2,5]{4,3,2,1,0:T(2,128)} %bitcast.14, s32[1,4]{1,0:T(1,128)} %bitcast.15, bf16[4,256,128]{2,1,0:T(8,128)(2,1)} %bitcast.12, bf16[4,5,128,128]{3,2,1,0:T(8,128)(2,1)} %bitcast.10, bf16[640,128]{1,0:T(8,128)(2,1)} %bitcast.13), custom_call_target="tpu_custom_call" | custom-call | tf_op jit(solution)/shard_map/zip_up/pallas_call | solution.py:328
  53.9 1.8 %copy.9 = bf16[1,4,128,2,128]{4,3,2,1,0:T(2,128)(2,1)} copy(bf16[1,4,128,2,128]{4,3,2,1,0:T(2,128)(2,1)} %bitcast.11) | data formatting | bytes 524288
  55.7 2.0 %copy.10 = bf16[1,4,128,5,128]{4,2,3,1,0:T(8,128)(2,1)} copy(bf16[1,4,128,5,128]{4,2,3,1,0:T(8,128)(2,1)} %bitcast.9) | data formatting | bytes 1310720

commit v3 on v2

--- a/solution.py
+++ b/solution.py
@@ -11,6 +11,7 @@
 WB = len(CHARGES)
 DS = 128
 ROWS = 8
+EARLY = 3
 MESH = pl.DeviceIdType.MESH
 F32 = jnp.float32
 BF16 = jnp.bfloat16
@@ -102,8 +103,8 @@
     sites, sectors,
     mpo_in, ranks_in, blocks_in, carry_in, sketch_in,
     sites_out, carry_out,
-    mpo, ranks, blk, sk, car, sent, below, iso, coupled, plain, work, inverse,
-    share_sem, blk_sem, sk_sem, pass_sem, load_sem, t_send, t_recv, o_send, o_recv,
+    mpo, ranks, blk, sk, car, sent, below, iso, coupled, plain, work, inverse, base, early, frames, made,
+    share_sem, blk_sem, sk_sem, pass_sem, load_sem, t_send, t_recv, o_send, o_recv, e_send, e_recv, m_sem,
 ):
     c = lax.axis_index("chain")
     p = lax.axis_index("block")
@@ -130,7 +131,21 @@
         pl.semaphore_signal(barrier, inc=1, device_id={"chain": lax.rem(c + d, sites)}, device_id_type=MESH)
     pl.semaphore_signal(barrier, inc=1, device_id=up, device_id_type=MESH)
     pl.semaphore_signal(barrier, inc=1, device_id=down, device_id_type=MESH)
-    pl.semaphore_wait(barrier, sites + 1)
+    last = sites - 1
+
+    @pl.when(c == last)
+    def _():
+        for a in range(last):
+            to = {"chain": a, "block": down["block"]}
+            pl.semaphore_signal(barrier, inc=1, device_id=to, device_id_type=MESH)
+
+    @pl.when(c == last)
+    def _():
+        pl.semaphore_wait(barrier, sites + 1)
+
+    @pl.when(c != last)
+    def _():
+        pl.semaphore_wait(barrier, sites + 2)
 
     def share(d, which):
         peer = lax.rem(c + d, sites)
@@ -193,10 +208,7 @@
                     coupled[t, pl.ds(w * DS, DS), pl.ds(v * DS, DS)] = (own[s] * weight).astype(BF16)
 
     share_blocks()
-
-    @pl.when(c == 0)
-    def _():
-        share_sketch()
+    share_sketch()
 
     for t in range(2):
         for w in range(WB):
@@ -208,23 +220,47 @@
     pass_on(0)
     prepare(0)
 
-    def output(k, which):
-        return (iso.at[k], sites_out.at[c]) if which == 0 else (car.at[k + 1], carry_out.at[c])
+    rest = pl.ds(EARLY, WB - EARLY)
 
     def outgoing(k, which):
-        return remote(*output(k, which), o_send.at[k, which], o_recv.at[c, which], {"chain": k})
+        if which == 0:
+            ends = iso.at[k], sites_out.at[c]
+        else:
+            ends = car.at[k + 1], carry_out.at[c]
+        return remote(*ends, o_send.at[k, which], o_recv.at[c, which], {"chain": k})
+
+    def final(which, peer):
+        if which == 0:
+            ends = iso.at[last], frames.at[peer]
+        else:
+            ends = car.at[sites, rest], carry_out.at[peer, rest]
+        return remote(*ends, o_send.at[last, which], o_recv.at[peer, which], {"chain": last})
 
     def kept(k, which):
-        return pltpu.make_async_copy(*output(k, which), o_send.at[k, which])
+        if which == 0:
+            return pltpu.make_async_copy(iso.at[k], sites_out.at[c], o_send.at[k, 0])
+        return pltpu.make_async_copy(car.at[k + 1], carry_out.at[c], o_send.at[k, 1])
+
+    def ahead(which, peer):
+        cut = pl.ds(0, EARLY)
+        if which == 0:
+            src, to = base, {"chain": last}
+        else:
+            src, to = sent.at[last, cut], {"chain": last, "block": up["block"]}
+        return remote(src, early.at[peer, which], e_send.at[which], e_recv.at[peer, which], to)
 
     def deliver(k, which):
         @pl.when(c == k)
         def _():
             kept(k, which).start()
 
-        @pl.when(c != k)
+        @pl.when(jnp.logical_and(c != k, k < last))
         def _():
             outgoing(k, which).start()
+
+        @pl.when(jnp.logical_and(c != k, k == last))
+        def _():
+            final(which, c).start()
 
     row_ids = lax.broadcasted_iota(jnp.int32, (DS, DS), 0)
     column_ids = lax.broadcasted_iota(jnp.int32, (DS, DS), 1)
@@ -244,7 +280,20 @@
             for v in range(v0, v1):
                 sent[k, v] = rows[:, (v - v0) * DS : (v - v0 + 1) * DS]
             raised(k, part).start()
+        hand_on = jnp.logical_and(k == last, c != last)
+
+        @pl.when(hand_on)
+        def _():
+            ahead(1, c).start()
+
         terms = dot(carried, coupled[0]).astype(BF16)
+
+        @pl.when(hand_on)
+        def _():
+            for v in range(EARLY):
+                base[v] = terms[:, v * DS : (v + 1) * DS]
+            ahead(0, c).start()
+
         arrived(sk.at[k], sk_sem.at[k])
         tests = sk[k].T
         rank = jnp.sum(jnp.where(site_ids == k, ranks[...].astype(F32), 0.0), axis=1, keepdims=True)
@@ -256,36 +305,27 @@
             for later in range(1, sites):
                 pass_on(later)
 
-        @pl.when(jnp.logical_and(k == 0, c > 0))
-        def _():
-            share_sketch()
-
         for part in range(len(CUTS)):
             raised(k, part).wait_recv()
         lower = jnp.concatenate([below[k, v] for v in range(WB)], axis=1)
         y1 = jnp.where(rows_f < upper_rank, dot(tests, lower, NT), 0.0)
-        high, low = halves(jnp.concatenate([y0, y1], axis=1))
-        gram = dot(
-            jnp.concatenate([high, high, low], axis=1), jnp.concatenate([high, low, high], axis=1), NT
-        )
+        y = jnp.concatenate([y0, y1], axis=1).astype(BF16)
+        gram = dot(y, y, NT)
         ridge = jnp.where(rows_f < rank, DS / 4.0, 1.0)
         work[:, :DS] = gram + jnp.where(row_ids == column_ids, ridge, 0.0)
         work[:, DS:] = jnp.where(row_ids == column_ids, 1.0, 0.0)
         invert_factor(work, inverse)
 
         inv_high, inv_low = halves(inverse[...])
-        frame = dot(
-            jnp.concatenate([inv_high, inv_low, inv_high], axis=1),
-            jnp.concatenate([high, high, low], axis=0),
-        )
+        frame = dot(jnp.concatenate([inv_high, inv_low], axis=1), jnp.concatenate([y, y], axis=0))
+        plain[0, pl.ds(0, DS, stride=2), :] = frame[:, :DS]
+        plain[0, pl.ds(1, DS, stride=2), :] = frame[:, DS:]
+        iso[k] = plain[0].astype(BF16)
+        deliver(k, 0)
         new = dot(frame.astype(BF16), jnp.concatenate([terms, lower], axis=0)).astype(BF16)
         for v in range(WB):
             car[k + 1, v] = new[:, v * DS : (v + 1) * DS]
         deliver(k, 1)
-        plain[0, pl.ds(0, DS, stride=2), :] = frame[:, :DS]
-        plain[0, pl.ds(1, DS, stride=2), :] = frame[:, DS:]
-        iso[k] = plain[0].astype(BF16)
-        deliver(k, 0)
 
         @pl.when(k + 1 < sites)
         def _():
@@ -311,12 +351,56 @@
         @pl.when(c != k)
         def _():
             for which in range(2):
-                outgoing(k, which).wait_send()
-
-    for d in range(1, sites):
-        peer = lax.rem(c + d, sites)
-        remote(iso.at[0], sites_out.at[peer], o_send.at[0, 0], o_recv.at[peer, 0], {"chain": peer}).wait_recv()
-        remote(car.at[1], carry_out.at[peer], o_send.at[0, 1], o_recv.at[peer, 1], {"chain": peer}).wait_recv()
+                (outgoing(k, which) if k < last else final(which, c)).wait_send()
+
+    @pl.when(c != last)
+    def _():
+        for which in range(2):
+            ahead(which, c).wait_send()
+        for d in range(1, sites):
+            peer = lax.rem(c + d, sites)
+            to = {"chain": peer}
+            remote(iso.at[0], sites_out.at[peer], o_send.at[0, 0], o_recv.at[peer, 0], to).wait_recv()
+            remote(car.at[1], carry_out.at[peer], o_send.at[0, 1], o_recv.at[peer, 1], to).wait_recv()
+
+    @pl.when(c == last)
+    def _():
+        placed = [
+            (
+                pltpu.make_async_copy(frames.at[a], sites_out.at[a], m_sem.at[a, 0]),
+                pltpu.make_async_copy(made.at[a], carry_out.at[a, pl.ds(0, EARLY)], m_sem.at[a, 1]),
+            )
+            for a in range(last)
+        ]
+        for a in range(last):
+            ahead(0, a).wait_recv()
+            ahead(1, a).wait_recv()
+            final(0, a).wait_recv()
+            placed[a][0].start()
+            plain[0] = frames[a].astype(F32)
+            frame = jnp.concatenate([plain[0, pl.ds(t, DS, stride=2), :] for t in range(2)], axis=1).astype(BF16)
+            rows = jnp.concatenate(
+                [jnp.concatenate([early[a, t, v] for v in range(EARLY)], axis=1) for t in range(2)], axis=0
+            )
+            new = dot(frame, rows).astype(BF16)
+            for v in range(EARLY):
+                made[a, v] = new[:, v * DS : (v + 1) * DS]
+            placed[a][1].start()
+        for a in range(last):
+            final(1, a).wait_recv()
+            for copy in placed[a]:
+                copy.wait()
+
+
+def keep(sites_in, carry_in, sites_out, carry_out, sem):
+    copies = (
+        pltpu.make_async_copy(carry_in, carry_out, sem.at[0]),
+        pltpu.make_async_copy(sites_in, sites_out, sem.at[1]),
+    )
+    for copy in copies:
+        copy.start()
+    for copy in copies:
+        copy.wait()
 
 
 def per_device(site_blocks, left_carry, mpo, sketch, ranks):
@@ -339,7 +423,7 @@
             pl.BlockSpec(memory_space=pltpu.HBM),
             pl.BlockSpec(memory_space=pltpu.HBM),
         ],
-        out_specs=(pl.BlockSpec(memory_space=pltpu.HBM), pl.BlockSpec(memory_space=pltpu.HBM)),
+        out_specs=(pl.BlockSpec(memory_space=pl.ANY), pl.BlockSpec(memory_space=pl.ANY)),
         scratch_shapes=[
             vmem(mpo.shape[:2] + (2, 2, WB), F32),
             vmem((1, sites), jnp.int32),
@@ -353,6 +437,10 @@
             vmem((3, 2 * DS, DS), F32),
             vmem((DS, 2 * DS), F32),
             vmem((DS, DS), F32),
+            vmem((EARLY, DS, DS), BF16),
+            vmem((sites, 2, EARLY, DS, DS), BF16),
+            vmem((sites, 2 * DS, DS), BF16),
+            vmem((sites, EARLY, DS, DS), BF16),
             dma((2, sites)),
             dma((sites, 3)),
             dma((sites,)),
@@ -362,17 +450,32 @@
             dma((sites, 2)),
             dma((sites, 2)),
             dma((sites, 2)),
+            dma((2,)),
+            dma((sites, 2)),
+            dma((sites, 2)),
         ],
         compiler_params=pltpu.CompilerParams(
-            collective_id=0, has_side_effects=True, vmem_limit_bytes=60 * 2**20
+            collective_id=0, has_side_effects=True, vmem_limit_bytes=40 * 2**20
         ),
-    )(
+    )(*(pltpu.with_memory_space_constraint(x, pltpu.HBM) for x in (
         jnp.transpose(mpo, (0, 1, 3, 4, 2)),
         jnp.transpose(ranks),
         site_blocks.reshape(states, 2 * DS, DS),
         jnp.transpose(left_carry, (0, 2, 1, 3)),
         sketch.reshape(WB * DS, DS),
-    )
+    )))
+    new_sites, carries = pl.pallas_call(
+        keep,
+        name="keep",
+        out_shape=(
+            jax.ShapeDtypeStruct(new_sites.shape, BF16),
+            jax.ShapeDtypeStruct(carries.shape, BF16),
+        ),
+        in_specs=[pl.BlockSpec(memory_space=pl.ANY)] * 2,
+        out_specs=(pl.BlockSpec(memory_space=pltpu.HBM), pl.BlockSpec(memory_space=pltpu.HBM)),
+        scratch_shapes=[dma((2,))],
+        compiler_params=pltpu.CompilerParams(vmem_limit_bytes=2**20),
+    )(new_sites, carries)
     return (
         new_sites.reshape(1, states, DS, 2, DS),
         jnp.transpose(carries, (0, 2, 1, 3))[None],

time: 57.9 us -> 53.3 us (0.921)
  local copies, waits for them, and re-layouts: 3.82 us -> 0 us
  Pallas kernels: 53.2 us -> 52.6 us
    unnamed x2 -> x0, local copies, waits for them, and re-layouts: 3.82 us -> none
    pallas_call x1, Pallas kernels: 53.2 us -> 51.7 us  [per_device(): pl.pallas_call(functools.partial(kernel, sites, sectors), name='zip_up',...]
    pallas_call x0 -> x1, Pallas kernels: none -> 0.94 us  [per_device(): pl.pallas_call(keep, name='keep', out_shape=(jax.ShapeDtypeStruct(new_sit...]
where the time goes in v3:
time: 53.3 us; the launch traced here: 53.2 us
  Pallas kernels  52.6 us (99%)
  between operations  0.64 us (1%)
    pallas_call x1, Pallas kernels, per_device(): pl.pallas_call(functools.partial(kernel, sites, sectors), name='zip_up',...  51.7 us

profile of v3, /device:TPU:24, one launch (start us, length us, event | category | flops | bytes accessed | tf_op | source)
XLA Modules:
  0.0 53.2 jit_solution(4782840521333502469)
XLA Ops:
  0.6 51.7 %zip_up.1 = (bf16[4,256,128]{2,1,0:T(8,128)(2,1)S(1)}, bf16[4,5,128,128]{3,2,1,0:T(8,128)(2,1)S(1)}) custom-call(f32[4,5,2,2,5]{4,3,2,1,0:T(2,128)} %bitcast.12, s32[1,4]{1,0:T(1,128)} %bitcast.13, bf16[4,256,128]{2,1,0:T(8,128)(2,1)} %bitcast.10, bf16[4,5,128,128]{3,2,1,0:T(8,128)(2,1)} %bitcast.9, bf16[640,128]{1,0:T(8,128)(2,1)} %bitcast.11), custom_call_target="tpu_custom_call" | custom-call | tf_op jit(solution)/shard_map/zip_up/pallas_call | solution.py:412
  52.3 0.9 %keep.1 = (bf16[4,256,128]{2,1,0:T(8,128)(2,1)}, bf16[4,5,128,128]{3,2,1,0:T(8,128)(2,1)}) custom-call(bf16[4,256,128]{2,1,0:T(8,128)(2,1)S(1)} %get-tuple-element.6.sites_in, bf16[4,5,128,128]{3,2,1,0:T(8,128)(2,1)S(1)} %get-tuple-element.7.carry_in), custom_call_target="tpu_custom_call" | custom-call | tf_op jit(solution)/shard_map/keep/pallas_call | solution.py:467

commit v4 on v3

--- a/solution.py
+++ b/solution.py
@@ -205,7 +205,7 @@
                         weight = weight * bottom
                     elif where == 2:
                         weight = weight * (top if s == 0 else below_top)
-                    coupled[t, pl.ds(w * DS, DS), pl.ds(v * DS, DS)] = (own[s] * weight).astype(BF16)
+                    coupled[lax.rem(k, 2), t, pl.ds(w * DS, DS), pl.ds(v * DS, DS)] = (own[s] * weight).astype(BF16)
 
     share_blocks()
     share_sketch()
@@ -214,7 +214,8 @@
         for w in range(WB):
             for v in range(WB):
                 if t - CHARGES[v] + CHARGES[w] not in (0, 1):
-                    coupled[t, pl.ds(w * DS, DS), pl.ds(v * DS, DS)] = jnp.zeros((DS, DS), BF16)
+                    for turn in range(2):
+                        coupled[turn, t, pl.ds(w * DS, DS), pl.ds(v * DS, DS)] = jnp.zeros((DS, DS), BF16)
     for load in loads:
         load.wait()
     pass_on(0)
@@ -276,7 +277,7 @@
     def step(k, carry):
         carried = jnp.concatenate([car[k, w] for w in range(WB)], axis=1)
         for part, (v0, v1) in enumerate(CUTS):
-            rows = dot(carried, coupled[1, :, pl.ds(v0 * DS, (v1 - v0) * DS)]).astype(BF16)
+            rows = dot(carried, coupled[lax.rem(k, 2), 1, :, pl.ds(v0 * DS, (v1 - v0) * DS)]).astype(BF16)
             for v in range(v0, v1):
                 sent[k, v] = rows[:, (v - v0) * DS : (v - v0 + 1) * DS]
             raised(k, part).start()
@@ -286,7 +287,7 @@
         def _():
             ahead(1, c).start()
 
-        terms = dot(carried, coupled[0]).astype(BF16)
+        terms = dot(carried, coupled[lax.rem(k, 2), 0]).astype(BF16)
 
         @pl.when(hand_on)
         def _():
@@ -304,6 +305,10 @@
         def _():
             for later in range(1, sites):
                 pass_on(later)
+
+        @pl.when(jnp.logical_and(k > 0, k + 1 < sites))
+        def _():
+            prepare(k + 1)
 
         for part in range(len(CUTS)):
             raised(k, part).wait_recv()
@@ -327,9 +332,9 @@
             car[k + 1, v] = new[:, v * DS : (v + 1) * DS]
         deliver(k, 1)
 
-        @pl.when(k + 1 < sites)
-        def _():
-            prepare(k + 1)
+        @pl.when(k == 0)
+        def _():
+            prepare(1)
 
         return carry
 
@@ -433,7 +438,7 @@
             vmem((sites, WB, DS, DS), BF16),
             vmem((sites, WB, DS, DS), BF16),
             vmem((sites, 2 * DS, DS), BF16),
-            vmem((2, WB * DS, WB * DS), BF16),
+            vmem((2, 2, WB * DS, WB * DS), BF16),
             vmem((3, 2 * DS, DS), F32),
             vmem((DS, 2 * DS), F32),
             vmem((DS, DS), F32),

time: 53.3 us -> 52.1 us (0.977)
  Pallas kernels: 52.6 us -> 51.3 us
    pallas_call x1, Pallas kernels: 51.7 us -> 50.4 us  [per_device(): pl.pallas_call(functools.partial(kernel, sites, sectors), name='zip_up',...]
where the time goes in v4:
time: 52.1 us; the launch traced here: 52 us
  Pallas kernels  51.3 us (98%)
  between operations  0.64 us (1%)
    pallas_call x1, Pallas kernels, per_device(): pl.pallas_call(functools.partial(kernel, sites, sectors), name='zip_up',...  50.4 us

profile of v4, /device:TPU:24, one launch (start us, length us, event | category | flops | bytes accessed | tf_op | source)
XLA Modules:
  0.0 52.0 jit_solution(14885104122344262978)
XLA Ops:
  0.6 50.4 %zip_up.1 = (bf16[4,256,128]{2,1,0:T(8,128)(2,1)S(1)}, bf16[4,5,128,128]{3,2,1,0:T(8,128)(2,1)S(1)}) custom-call(f32[4,5,2,2,5]{4,3,2,1,0:T(2,128)} %bitcast.12, s32[1,4]{1,0:T(1,128)} %bitcast.13, bf16[4,256,128]{2,1,0:T(8,128)(2,1)} %bitcast.10, bf16[4,5,128,128]{3,2,1,0:T(8,128)(2,1)} %bitcast.9, bf16[640,128]{1,0:T(8,128)(2,1)} %bitcast.11), custom_call_target="tpu_custom_call" | custom-call | tf_op jit(solution)/shard_map/zip_up/pallas_call | solution.py:417
  51.0 0.9 %keep.1 = (bf16[4,256,128]{2,1,0:T(8,128)(2,1)}, bf16[4,5,128,128]{3,2,1,0:T(8,128)(2,1)}) custom-call(bf16[4,256,128]{2,1,0:T(8,128)(2,1)S(1)} %get-tuple-element.6.sites_in, bf16[4,5,128,128]{3,2,1,0:T(8,128)(2,1)S(1)} %get-tuple-element.7.carry_in), custom_call_target="tpu_custom_call" | custom-call | tf_op jit(solution)/shard_map/keep/pallas_call | solution.py:472

commit v5 on v4

--- a/solution.py
+++ b/solution.py
@@ -306,19 +306,22 @@
             for later in range(1, sites):
                 pass_on(later)
 
+        work[:, DS:] = jnp.where(row_ids == column_ids, 1.0, 0.0)
+        ridge = jnp.where(row_ids == column_ids, jnp.where(rows_f < rank, DS / 4.0, 1.0), 0.0)
         @pl.when(jnp.logical_and(k > 0, k + 1 < sites))
         def _():
             prepare(k + 1)
 
-        for part in range(len(CUTS)):
+        y1 = 0.0
+        for part, (v0, v1) in enumerate(CUTS):
             raised(k, part).wait_recv()
+            rows = jnp.concatenate([below[k, v] for v in range(v0, v1)], axis=1)
+            y1 = y1 + dot(tests[:, v0 * DS : v1 * DS], rows, NT)
+        y1 = jnp.where(rows_f < upper_rank, y1, 0.0)
         lower = jnp.concatenate([below[k, v] for v in range(WB)], axis=1)
-        y1 = jnp.where(rows_f < upper_rank, dot(tests, lower, NT), 0.0)
         y = jnp.concatenate([y0, y1], axis=1).astype(BF16)
         gram = dot(y, y, NT)
-        ridge = jnp.where(rows_f < rank, DS / 4.0, 1.0)
-        work[:, :DS] = gram + jnp.where(row_ids == column_ids, ridge, 0.0)
-        work[:, DS:] = jnp.where(row_ids == column_ids, 1.0, 0.0)
+        work[:, :DS] = gram + ridge
         invert_factor(work, inverse)
 
         inv_high, inv_low = halves(inverse[...])
@@ -377,7 +380,7 @@
             )
             for a in range(last)
         ]
-        for a in range(last):
+        for a in sorted(range(last), key=lambda a: min(last - a, a + 1)):
             ahead(0, a).wait_recv()
             ahead(1, a).wait_recv()
             final(0, a).wait_recv()

time: 52.1 us -> 52.4 us (level)
  no operation moved by 1% of the time
where the time goes in v5:
time: 52.4 us; the launch traced here: 52.3 us
  Pallas kernels  51.7 us (99%)
  between operations  0.64 us (1%)
    pallas_call x1, Pallas kernels, per_device(): pl.pallas_call(functools.partial(kernel, sites, sectors), name='zip_up',...  50.7 us

profile of v5, /device:TPU:24, one launch (start us, length us, event | category | flops | bytes accessed | tf_op | source)
XLA Modules:
  0.0 52.3 jit_solution(8537402850840658855)
XLA Ops:
  0.6 50.7 %zip_up.1 = (bf16[4,256,128]{2,1,0:T(8,128)(2,1)S(1)}, bf16[4,5,128,128]{3,2,1,0:T(8,128)(2,1)S(1)}) custom-call(f32[4,5,2,2,5]{4,3,2,1,0:T(2,128)} %bitcast.12, s32[1,4]{1,0:T(1,128)} %bitcast.13, bf16[4,256,128]{2,1,0:T(8,128)(2,1)} %bitcast.10, bf16[4,5,128,128]{3,2,1,0:T(8,128)(2,1)} %bitcast.9, bf16[640,128]{1,0:T(8,128)(2,1)} %bitcast.11), custom_call_target="tpu_custom_call" | custom-call | tf_op jit(solution)/shard_map/zip_up/pallas_call | solution.py:420
  51.4 0.9 %keep.1 = (bf16[4,256,128]{2,1,0:T(8,128)(2,1)}, bf16[4,5,128,128]{3,2,1,0:T(8,128)(2,1)}) custom-call(bf16[4,256,128]{2,1,0:T(8,128)(2,1)S(1)} %get-tuple-element.6.sites_in, bf16[4,5,128,128]{3,2,1,0:T(8,128)(2,1)S(1)} %get-tuple-element.7.carry_in), custom_call_target="tpu_custom_call" | custom-call | tf_op jit(solution)/shard_map/keep/pallas_call | solution.py:475

commit v6 on v4

--- a/solution.py
+++ b/solution.py
@@ -161,10 +161,10 @@
     ORDER = (1, sites - 1) + tuple(range(2, sites - 1))
 
     def share_blocks():
+        for which in range(2):
+            passed(c, which, blocks_in.at[c]).start()
         for d in ORDER:
             share(d, 0).start()
-        for which in range(2):
-            passed(c, which, blocks_in.at[c]).start()
 
     def share_sketch():
         for d in ORDER:
@@ -377,7 +377,7 @@
             )
             for a in range(last)
         ]
-        for a in range(last):
+        for a in sorted(range(last), key=lambda a: min(last - a, a + 1)):
             ahead(0, a).wait_recv()
             ahead(1, a).wait_recv()
             final(0, a).wait_recv()

time: 52.1 us -> 52.2 us (level)
  no operation moved by 1% of the time
where the time goes in v6:
time: 52.2 us; the launch traced here: 52.1 us
  Pallas kernels  51.5 us (99%)
  between operations  0.64 us (1%)
    pallas_call x1, Pallas kernels, per_device(): pl.pallas_call(functools.partial(kernel, sites, sectors), name='zip_up',...  50.6 us

profile of v6, /device:TPU:24, one launch (start us, length us, event | category | flops | bytes accessed | tf_op | source)
XLA Modules:
  0.0 52.1 jit_solution(5547786500618447652)
XLA Ops:
  0.6 50.6 %zip_up.1 = (bf16[4,256,128]{2,1,0:T(8,128)(2,1)S(1)}, bf16[4,5,128,128]{3,2,1,0:T(8,128)(2,1)S(1)}) custom-call(f32[4,5,2,2,5]{4,3,2,1,0:T(2,128)} %bitcast.12, s32[1,4]{1,0:T(1,128)} %bitcast.13, bf16[4,256,128]{2,1,0:T(8,128)(2,1)} %bitcast.10, bf16[4,5,128,128]{3,2,1,0:T(8,128)(2,1)} %bitcast.9, bf16[640,128]{1,0:T(8,128)(2,1)} %bitcast.11), custom_call_target="tpu_custom_call" | custom-call | tf_op jit(solution)/shard_map/zip_up/pallas_call | solution.py:417
  51.2 0.9 %keep.1 = (bf16[4,256,128]{2,1,0:T(8,128)(2,1)}, bf16[4,5,128,128]{3,2,1,0:T(8,128)(2,1)}) custom-call(bf16[4,256,128]{2,1,0:T(8,128)(2,1)S(1)} %get-tuple-element.6.sites_in, bf16[4,5,128,128]{3,2,1,0:T(8,128)(2,1)S(1)} %get-tuple-element.7.carry_in), custom_call_target="tpu_custom_call" | custom-call | tf_op jit(solution)/shard_map/keep/pallas_call | solution.py:472
